TPU v7x, 512 devices: a whole 4x4x16 slice. The times are simulated.
512 devices in a mesh: blk: 32 (over y, z_lo), shard: 16 (over x, z_hi, core).
Axes of the slice: x: 4, y: 4, z: 16 (z_hi: 2, z_lo: 8; z = z_hi * 8 + z_lo), core: 2. Of those that a mesh axis runs over, the one named last changes fastest.
Arguments:
- weights: bfloat16 [32, 8192, 2048], P('blk', 'shard'), may hold values from -90 to 90
- warm_factor: float32 [32, 32, 2048], P('blk'), may hold values from -6 to 6
Outputs:
- new_weights: bfloat16 [32, 8192, 2048], P('blk', 'shard')
- new_factor: float32 [32, 32, 2048], P('blk', None, 'shard')
All inputs are finite; a program needn't handle non-finite values.
Results may differ from a plain program's by a relative error of at most 0.012.
Values may be sent and summed in bfloat16 or wider, within the bound.
A program may use at most 64 MiB of HBM per device.

v0:
```python
import jax
import jax.numpy as jnp
from jax import lax
from jax.sharding import PartitionSpec as P

POWER = 4


MIXING = 1.0 / 3.0


def passed_along(value, axis, by):
    peers = lax.axis_size(axis)
    return lax.ppermute(value, axis, [(i, (i + by) % peers) for i in range(peers)])


def sent_to_all(value, axis):
    peers = lax.axis_size(axis)
    return lax.all_to_all(
        jnp.broadcast_to(value[None], (peers, *value.shape)), axis, 0, 0, tiled=True
    )


def of_everyone(value, axis):
    everything = sent_to_all(value, axis)
    return jnp.sum(everything, axis=0)


def in_blocks(value, dim, peers):
    before, after = (value.shape[:dim], value.shape[dim + 1 :])
    return jnp.moveaxis(value.reshape(*before, peers, -1, *after), dim, 0)


def summed_on_arrival(value, axis, dim):
    pieces = in_blocks(value, dim, lax.axis_size(axis))
    arrived = lax.all_to_all(pieces, axis, split_axis=0, concat_axis=0, tiled=True)
    return arrived.astype(jnp.float32).sum(axis=0)


def in_order(pieces, dim):
    dims = list(pieces.shape[1:])
    dims[dim] *= pieces.shape[0]
    return jnp.moveaxis(pieces, 0, dim).reshape(dims)


def collect(value, axis, dim):
    pieces = sent_to_all(value, axis)
    return in_order(pieces, dim)


def lower_solve(lower_factor, right_hand):
    return jax.scipy.linalg.solve_triangular(lower_factor, right_hand, lower=True)


def on_device(weights, warm_factor):
    local_weight = weights[0]
    own_factor = warm_factor[0]
    own_rounded = own_factor.astype(jnp.bfloat16)
    prior_rounded = passed_along(own_rounded, "blk", 1)
    rounded = jnp.stack([own_rounded, prior_rounded])
    width_piece = local_weight.shape[1] // lax.axis_size("shard")
    own_piece = jnp.stack([own_factor, own_factor])[:, :, :width_piece]
    left_rows = jnp.zeros((2, own_factor.shape[0], local_weight.shape[0]), jnp.bfloat16)
    for iteration in range(POWER):
        products = jnp.einsum(
            "ekc,rc->ekr", rounded, local_weight, preferred_element_type=jnp.float32
        )
        from_next = passed_along(products[1], "blk", -1)
        from_prior = passed_along(products[0], "blk", 1)
        raw_factor = jnp.stack([products[0] - from_next, from_prior - products[1]])
        gram = jnp.einsum("ekr,elr->ekl", raw_factor, raw_factor, precision=lax.Precision.HIGHEST)
        gram = of_everyone(gram, "shard")
        lower_factor = jnp.linalg.cholesky(gram)
        basis = jax.vmap(lower_solve)(lower_factor, raw_factor)
        left_rows = basis.astype(jnp.bfloat16)
        partials = jnp.einsum(
            "ekr,rc->ekc", left_rows, local_weight, preferred_element_type=jnp.float32
        )
        summed = summed_on_arrival(partials.astype(jnp.bfloat16), "shard", 2)
        next_piece = passed_along(summed[1], "blk", -1)
        prior_piece = passed_along(summed[0], "blk", 1)
        own_piece = jnp.stack([summed[0] - next_piece, prior_piece - summed[1]])
        rounded = collect(own_piece.astype(jnp.bfloat16), "shard", 2)
    signed = jnp.concatenate([left_rows[1], -left_rows[0]], axis=0)
    factor_pair = jnp.concatenate([rounded[1], rounded[0]], axis=0)
    delta = jnp.einsum("jr,jc->rc", signed, factor_pair, preferred_element_type=jnp.float32)
    new_weight = (local_weight.astype(jnp.float32) + MIXING * delta).astype(jnp.bfloat16)
    return (new_weight[None], own_piece[0][None])


def solution(mesh):
    placed = (P("blk", "shard", None), P("blk", None, None))
    return jax.shard_map(
        on_device,
        mesh=mesh,
        in_specs=placed,
        out_specs=(P("blk", "shard", None), P("blk", None, "shard")),
        check_vma=False,
    )
```

profile of v0, /device:TPU:1, one launch (start us, length us, event | category | flops | bytes accessed | tf_op | source)
XLA Modules:
  0.0 478.9 jit_solution(16141631251116031138)
XLA Ops:
  1.6 4.4 collective-permute-start
  6.9 13.2 %collective-permute-done = bf16[32,2048]{1,0:T(8,128)(2,1)S(1)} collective-permute-done((bf16[32,2048]{1,0:T(8,128)(2,1)S(1)}, bf16[32,2048]{1,0:T(8,128)(2,1)S(1)}, u32[]{:S(2)}, u32[]{:S(2)}) %collective-permute-start) | collective-permute-done | bytes 131104 | tf_op jit(solution)/shard_map/ppermute | solution.py:14
  28.5 11.8 %collective-permute-done.2 = f32[32,512]{1,0:T(8,128)S(1)} collective-permute-done((f32[32,512]{1,0:T(8,128)S(1)}, f32[32,512]{1,0:T(8,128)S(1)}, u32[]{:S(2)}, u32[]{:S(2)}) %collective-permute-start.2) | collective-permute-done | bytes 65568 | tf_op jit(solution)/shard_map/ppermute | solution.py:14
  41.5 15.5 %all-to-all-start = ((f32[16,1,2048]{2,1,0:T(1,128)}), f32[16,1,2048]{2,1,0:T(1,128)S(1)}, u32[]{:S(2)}, u32[]{:S(2)}) async-start(f32[16,1,2048]{2,1,0:T(1,128)} %reshape.128), calls=%async_computation | async-start | bytes 262144 | tf_op jit(solution)/shard_map/all_to_all | solution.py:19
  57.1 14.8 %all-to-all-done = f32[16,1,2048]{2,1,0:T(1,128)S(1)} async-done(((f32[16,1,2048]{2,1,0:T(1,128)}), f32[16,1,2048]{2,1,0:T(1,128)S(1)}, u32[]{:S(2)}, u32[]{:S(2)}) %all-to-all-start) | async-done | bytes 131104 | tf_op jit(solution)/shard_map/all_to_all | solution.py:19
  73.7 5.9 %custom-call.12 = f32[2,32,32]{2,1,0:T(8,128)S(1)} custom-call(f32[2,32,32]{2,1,0:T(8,128)S(1)} %fusion.52), custom_call_target="Cholesky" | custom-call | tf_op jit(solution)/shard_map/jit(cholesky)/cholesky | solution.py:73
  79.8 4.9 %custom-call.13 = f32[2,1,32,32]{2,3,1,0:T(8,128)S(1)} custom-call(f32[2,1,32,32]{3,2,1,0:T(8,128)S(1)} %select_bitcast_fusion.3), custom_call_target="InvertDiagBlocksLowerTriangular" | custom-call | tf_op jit(solution)/shard_map/vmap(jit(_solve_triangular))/triangular_solve | solution.py:52
  85.6 20.2 %all_to_all.60 = bf16[16,2,32,128]{3,2,1,0:T(8,128)(2,1)S(1)} all-to-all(bf16[16,2,32,128]{3,2,1,0:T(8,128)(2,1)S(1)} %bitcast.240), channel_id=1, replica_groups=mesh['blk'=32,'shard'=16] {'shard'}, dimensions={0} | all-to-all | bytes 524288 | tf_op jit(solution)/shard_map/all_to_all | solution.py:36
  111.2 11.5 %collective-permute-done.4 = f32[32,128]{1,0:T(8,128)S(1)} collective-permute-done((f32[32,128]{1,0:T(8,128)S(1)}, f32[32,128]{1,0:T(8,128)S(1)}, u32[]{:S(2)}, u32[]{:S(2)}) %collective-permute-start.4) | collective-permute-done | bytes 16416 | tf_op jit(solution)/shard_map/ppermute | solution.py:14
  122.8 23.4 %all_to_all.61 = bf16[16,2,32,128]{3,2,1,0:T(8,128)(2,1)S(1)} all-to-all(bf16[16,2,32,128]{3,2,1,0:T(8,128)(2,1)S(1)} %broadcast_in_dim.23), channel_id=1, replica_groups=mesh['blk'=32,'shard'=16] {'shard'}, dimensions={0} | all-to-all | bytes 524288 | tf_op jit(solution)/shard_map/all_to_all | solution.py:19
  152.3 10.6 %collective-permute-done.6 = f32[32,512]{1,0:T(8,128)S(1)} collective-permute-done((f32[32,512]{1,0:T(8,128)S(1)}, f32[32,512]{1,0:T(8,128)S(1)}, u32[]{:S(2)}, u32[]{:S(2)}) %collective-permute-start.6) | collective-permute-done | bytes 65568 | tf_op jit(solution)/shard_map/ppermute | solution.py:14
  163.5 22.4 %all_to_all.62 = f32[16,1,2048]{2,1,0:T(1,128)S(1)} all-to-all(f32[16,1,2048]{2,1,0:T(1,128)S(1)} %reshape.130), channel_id=1, replica_groups=mesh['blk'=32,'shard'=16] {'shard'}, dimensions={0} | all-to-all | bytes 262144 | tf_op jit(solution)/shard_map/all_to_all | solution.py:19
  187.2 5.9 %custom-call.14 = f32[2,32,32]{2,1,0:T(8,128)S(1)} custom-call(f32[2,32,32]{2,1,0:T(8,128)S(1)} %fusion.50), custom_call_target="Cholesky" | custom-call | tf_op jit(solution)/shard_map/jit(cholesky)/cholesky | solution.py:73
  193.3 4.9 %custom-call.15 = f32[2,1,32,32]{2,3,1,0:T(8,128)S(1)} custom-call(f32[2,1,32,32]{3,2,1,0:T(8,128)S(1)} %select_bitcast_fusion.2), custom_call_target="InvertDiagBlocksLowerTriangular" | custom-call | tf_op jit(solution)/shard_map/vmap(jit(_solve_triangular))/triangular_solve | solution.py:52
  199.1 19.0 %all_to_all.63 = bf16[16,2,32,128]{3,2,1,0:T(8,128)(2,1)S(1)} all-to-all(bf16[16,2,32,128]{3,2,1,0:T(8,128)(2,1)S(1)} %bitcast.241), channel_id=1, replica_groups=mesh['blk'=32,'shard'=16] {'shard'}, dimensions={0} | all-to-all | bytes 524288 | tf_op jit(solution)/shard_map/all_to_all | solution.py:36
  223.5 9.9 %collective-permute-done.8 = f32[32,128]{1,0:T(8,128)S(1)} collective-permute-done((f32[32,128]{1,0:T(8,128)S(1)}, f32[32,128]{1,0:T(8,128)S(1)}, u32[]{:S(2)}, u32[]{:S(2)}) %collective-permute-start.8) | collective-permute-done | bytes 16416 | tf_op jit(solution)/shard_map/ppermute | solution.py:14
  233.5 24.2 %all_to_all.64 = bf16[16,2,32,128]{3,2,1,0:T(8,128)(2,1)S(1)} all-to-all(bf16[16,2,32,128]{3,2,1,0:T(8,128)(2,1)S(1)} %broadcast_in_dim.25), channel_id=1, replica_groups=mesh['blk'=32,'shard'=16] {'shard'}, dimensions={0} | all-to-all | bytes 524288 | tf_op jit(solution)/shard_map/all_to_all | solution.py:19
  263.8 10.4 %collective-permute-done.10 = f32[32,512]{1,0:T(8,128)S(1)} collective-permute-done((f32[32,512]{1,0:T(8,128)S(1)}, f32[32,512]{1,0:T(8,128)S(1)}, u32[]{:S(2)}, u32[]{:S(2)}) %collective-permute-start.10) | collective-permute-done | bytes 65568 | tf_op jit(solution)/shard_map/ppermute | solution.py:14
  274.8 20.3 %all_to_all.65 = f32[16,1,2048]{2,1,0:T(1,128)S(1)} all-to-all(f32[16,1,2048]{2,1,0:T(1,128)S(1)} %reshape.132), channel_id=1, replica_groups=mesh['blk'=32,'shard'=16] {'shard'}, dimensions={0} | all-to-all | bytes 262144 | tf_op jit(solution)/shard_map/all_to_all | solution.py:19
  296.4 5.9 %custom-call.16 = f32[2,32,32]{2,1,0:T(8,128)S(1)} custom-call(f32[2,32,32]{2,1,0:T(8,128)S(1)} %fusion.48), custom_call_target="Cholesky" | custom-call | tf_op jit(solution)/shard_map/jit(cholesky)/cholesky | solution.py:73
  302.5 4.9 %custom-call.17 = f32[2,1,32,32]{2,3,1,0:T(8,128)S(1)} custom-call(f32[2,1,32,32]{3,2,1,0:T(8,128)S(1)} %select_bitcast_fusion.1), custom_call_target="InvertDiagBlocksLowerTriangular" | custom-call | tf_op jit(solution)/shard_map/vmap(jit(_solve_triangular))/triangular_solve | solution.py:52
  308.3 20.3 %all_to_all.66 = bf16[16,2,32,128]{3,2,1,0:T(8,128)(2,1)S(1)} all-to-all(bf16[16,2,32,128]{3,2,1,0:T(8,128)(2,1)S(1)} %bitcast.242), channel_id=1, replica_groups=mesh['blk'=32,'shard'=16] {'shard'}, dimensions={0} | all-to-all | bytes 524288 | tf_op jit(solution)/shard_map/all_to_all | solution.py:36
  334.0 9.9 %collective-permute-done.12 = f32[32,128]{1,0:T(8,128)S(1)} collective-permute-done((f32[32,128]{1,0:T(8,128)S(1)}, f32[32,128]{1,0:T(8,128)S(1)}, u32[]{:S(2)}, u32[]{:S(2)}) %collective-permute-start.12) | collective-permute-done | bytes 16416 | tf_op jit(solution)/shard_map/ppermute | solution.py:14
  344.0 21.8 %all_to_all.67 = bf16[16,2,32,128]{3,2,1,0:T(8,128)(2,1)S(1)} all-to-all(bf16[16,2,32,128]{3,2,1,0:T(8,128)(2,1)S(1)} %broadcast_in_dim.27), channel_id=1, replica_groups=mesh['blk'=32,'shard'=16] {'shard'}, dimensions={0} | all-to-all | bytes 524288 | tf_op jit(solution)/shard_map/all_to_all | solution.py:19
  372.1 10.1 %collective-permute-done.14 = f32[32,512]{1,0:T(8,128)S(1)} collective-permute-done((f32[32,512]{1,0:T(8,128)S(1)}, f32[32,512]{1,0:T(8,128)S(1)}, u32[]{:S(2)}, u32[]{:S(2)}) %collective-permute-start.14) | collective-permute-done | bytes 65568 | tf_op jit(solution)/shard_map/ppermute | solution.py:14
  382.8 23.0 %all_to_all.68 = f32[16,1,2048]{2,1,0:T(1,128)S(1)} all-to-all(f32[16,1,2048]{2,1,0:T(1,128)S(1)} %reshape.134), channel_id=1, replica_groups=mesh['blk'=32,'shard'=16] {'shard'}, dimensions={0} | all-to-all | bytes 262144 | tf_op jit(solution)/shard_map/all_to_all | solution.py:19
  407.1 5.9 %custom-call.18 = f32[2,32,32]{2,1,0:T(8,128)S(1)} custom-call(f32[2,32,32]{2,1,0:T(8,128)S(1)} %fusion.46), custom_call_target="Cholesky" | custom-call | tf_op jit(solution)/shard_map/jit(cholesky)/cholesky | solution.py:73
  413.2 4.9 %custom-call.19 = f32[2,1,32,32]{2,3,1,0:T(8,128)S(1)} custom-call(f32[2,1,32,32]{3,2,1,0:T(8,128)S(1)} %select_bitcast_fusion), custom_call_target="InvertDiagBlocksLowerTriangular" | custom-call | tf_op jit(solution)/shard_map/vmap(jit(_solve_triangular))/triangular_solve | solution.py:52
  419.0 19.1 %all_to_all.69 = bf16[16,2,32,128]{3,2,1,0:T(8,128)(2,1)S(1)} all-to-all(bf16[16,2,32,128]{3,2,1,0:T(8,128)(2,1)S(1)} %bitcast.243), channel_id=1, replica_groups=mesh['blk'=32,'shard'=16] {'shard'}, dimensions={0} | all-to-all | bytes 524288 | tf_op jit(solution)/shard_map/all_to_all | solution.py:36
  444.9 8.4 %collective-permute-done.16 = f32[32,128]{1,0:T(8,128)S(1)} collective-permute-done((f32[32,128]{1,0:T(8,128)S(1)}, f32[32,128]{1,0:T(8,128)S(1)}, u32[]{:S(2)}, u32[]{:S(2)}) %collective-permute-start.16) | collective-permute-done | bytes 16416 | tf_op jit(solution)/shard_map/ppermute | solution.py:14
  454.7 6.0 %all-to-all-start.11 = ((bf16[16,2,32,128]{3,2,1,0:T(8,128)(2,1)}), bf16[16,2,32,128]{3,2,1,0:T(8,128)(2,1)S(1)}, u32[]{:S(2)}, u32[]{:S(2)}) async-start(bf16[16,2,32,128]{3,2,1,0:T(8,128)(2,1)} %broadcast_in_dim.29), calls=%async_computation.11 | async-start | bytes 524288 | tf_op jit(solution)/shard_map/all_to_all | solution.py:19
  460.7 15.9 %all-to-all-done.11 = bf16[16,2,32,128]{3,2,1,0:T(8,128)(2,1)S(1)} async-done(((bf16[16,2,32,128]{3,2,1,0:T(8,128)(2,1)}), bf16[16,2,32,128]{3,2,1,0:T(8,128)(2,1)S(1)}, u32[]{:S(2)}, u32[]{:S(2)}) %all-to-all-start.11) | async-done | bytes 262176 | tf_op jit(solution)/shard_map/all_to_all | solution.py:19
  (125 shorter events, 68.1 us)
Async XLA Ops:
  1.6 18.6 %collective-permute-start = (bf16[32,2048]{1,0:T(8,128)(2,1)S(1)}, bf16[32,2048]{1,0:T(8,128)(2,1)S(1)}, u32[]{:S(2)}, u32[]{:S(2)}) collective-permute-start(bf16[32,2048]{1,0:T(8,128)(2,1)S(1)} %convert_bitcast_fusion), channel_id=1, source_target_pairs={{0,16},{16,32},{32,48},{48,64},{64,80},{80,96},{96,112},{112,128},... | collective-permute-start | bytes 393224 | tf_op jit(solution)/shard_map/ppermute | solution.py:14
  22.5 62.5 %copy-start = (bf16[1,512,2048]{2,1,0:T(8,128)(2,1)S(1)}, bf16[1,512,2048]{2,1,0:T(8,128)(2,1)}, u32[]{:S(2)}) copy-start(bf16[1,512,2048]{2,1,0:T(8,128)(2,1)} %param.5) | copy-start | bytes 6291460
  22.5 5.9 %collective-permute-start.1 = (f32[32,512]{1,0:T(8,128)S(1)}, f32[32,512]{1,0:T(8,128)S(1)}, u32[]{:S(2)}, u32[]{:S(2)}) collective-permute-start(f32[32,512]{1,0:T(8,128)S(1)} %get-tuple-element.22), channel_id=1, source_target_pairs={{0,496},{16,0},{32,16},{48,32},{64,48},{80,64},{96,80},{112,96},{1... | collective-permute-start | bytes 196616 | tf_op jit(solution)/shard_map/ppermute | solution.py:14
  26.5 13.7 %collective-permute-start.2 = (f32[32,512]{1,0:T(8,128)S(1)}, f32[32,512]{1,0:T(8,128)S(1)}, u32[]{:S(2)}, u32[]{:S(2)}) collective-permute-start(f32[32,512]{1,0:T(8,128)S(1)} %get-tuple-element.23), channel_id=1, source_target_pairs={{0,16},{16,32},{32,48},{48,64},{64,80},{80,96},{96,112},{112,128},... | collective-permute-start | bytes 196616 | tf_op jit(solution)/shard_map/ppermute | solution.py:14
  41.5 30.4 %all-to-all-start = ((f32[16,1,2048]{2,1,0:T(1,128)}), f32[16,1,2048]{2,1,0:T(1,128)S(1)}, u32[]{:S(2)}, u32[]{:S(2)}) async-start(f32[16,1,2048]{2,1,0:T(1,128)} %reshape.128), calls=%async_computation | async-start | bytes 262144 | tf_op jit(solution)/shard_map/all_to_all | solution.py:19
  105.9 5.3 %collective-permute-start.3 = (f32[32,128]{1,0:T(8,128)S(1)}, f32[32,128]{1,0:T(8,128)S(1)}, u32[]{:S(2)}, u32[]{:S(2)}) collective-permute-start(f32[32,128]{1,0:T(8,128)S(1)} %get-tuple-element.39), channel_id=1, source_target_pairs={{0,496},{16,0},{32,16},{48,32},{64,48},{80,64},{96,80},{112,96},{1... | collective-permute-start | bytes 49160 | tf_op jit(solution)/shard_map/ppermute | solution.py:14
  107.8 14.9 %collective-permute-start.4 = (f32[32,128]{1,0:T(8,128)S(1)}, f32[32,128]{1,0:T(8,128)S(1)}, u32[]{:S(2)}, u32[]{:S(2)}) collective-permute-start(f32[32,128]{1,0:T(8,128)S(1)} %get-tuple-element.40), channel_id=1, source_target_pairs={{0,16},{16,32},{32,48},{48,64},{64,80},{80,96},{96,112},{112,128},... | collective-permute-start | bytes 49160 | tf_op jit(solution)/shard_map/ppermute | solution.py:14
  147.0 5.3 %collective-permute-start.5 = (f32[32,512]{1,0:T(8,128)S(1)}, f32[32,512]{1,0:T(8,128)S(1)}, u32[]{:S(2)}, u32[]{:S(2)}) collective-permute-start(f32[32,512]{1,0:T(8,128)S(1)} %get-tuple-element.18), channel_id=1, source_target_pairs={{0,496},{16,0},{32,16},{48,32},{64,48},{80,64},{96,80},{112,96},{1... | collective-permute-start | bytes 196616 | tf_op jit(solution)/shard_map/ppermute | solution.py:14
  148.9 14.0 %collective-permute-start.6 = (f32[32,512]{1,0:T(8,128)S(1)}, f32[32,512]{1,0:T(8,128)S(1)}, u32[]{:S(2)}, u32[]{:S(2)}) collective-permute-start(f32[32,512]{1,0:T(8,128)S(1)} %get-tuple-element.19), channel_id=1, source_target_pairs={{0,16},{16,32},{32,48},{48,64},{64,80},{80,96},{96,112},{112,128},... | collective-permute-start | bytes 196616 | tf_op jit(solution)/shard_map/ppermute | solution.py:14
  218.2 5.3 %collective-permute-start.7 = (f32[32,128]{1,0:T(8,128)S(1)}, f32[32,128]{1,0:T(8,128)S(1)}, u32[]{:S(2)}, u32[]{:S(2)}) collective-permute-start(f32[32,128]{1,0:T(8,128)S(1)} %get-tuple-element.35), channel_id=1, source_target_pairs={{0,496},{16,0},{32,16},{48,32},{64,48},{80,64},{96,80},{112,96},{1... | collective-permute-start | bytes 49160 | tf_op jit(solution)/shard_map/ppermute | solution.py:14
  220.1 13.3 %collective-permute-start.8 = (f32[32,128]{1,0:T(8,128)S(1)}, f32[32,128]{1,0:T(8,128)S(1)}, u32[]{:S(2)}, u32[]{:S(2)}) collective-permute-start(f32[32,128]{1,0:T(8,128)S(1)} %get-tuple-element.36), channel_id=1, source_target_pairs={{0,16},{16,32},{32,48},{48,64},{64,80},{80,96},{96,112},{112,128},... | collective-permute-start | bytes 49160 | tf_op jit(solution)/shard_map/ppermute | solution.py:14
  258.5 5.3 %collective-permute-start.9 = (f32[32,512]{1,0:T(8,128)S(1)}, f32[32,512]{1,0:T(8,128)S(1)}, u32[]{:S(2)}, u32[]{:S(2)}) collective-permute-start(f32[32,512]{1,0:T(8,128)S(1)} %get-tuple-element.14), channel_id=1, source_target_pairs={{0,496},{16,0},{32,16},{48,32},{64,48},{80,64},{96,80},{112,96},{1... | collective-permute-start | bytes 196616 | tf_op jit(solution)/shard_map/ppermute | solution.py:14
  260.4 13.8 %collective-permute-start.10 = (f32[32,512]{1,0:T(8,128)S(1)}, f32[32,512]{1,0:T(8,128)S(1)}, u32[]{:S(2)}, u32[]{:S(2)}) collective-permute-start(f32[32,512]{1,0:T(8,128)S(1)} %get-tuple-element.15), channel_id=1, source_target_pairs={{0,16},{16,32},{32,48},{48,64},{64,80},{80,96},{96,112},{112,128},... | collective-permute-start | bytes 196616 | tf_op jit(solution)/shard_map/ppermute | solution.py:14
  328.7 5.3 %collective-permute-start.11 = (f32[32,128]{1,0:T(8,128)S(1)}, f32[32,128]{1,0:T(8,128)S(1)}, u32[]{:S(2)}, u32[]{:S(2)}) collective-permute-start(f32[32,128]{1,0:T(8,128)S(1)} %get-tuple-element.31), channel_id=1, source_target_pairs={{0,496},{16,0},{32,16},{48,32},{64,48},{80,64},{96,80},{112,96},{1... | collective-permute-start | bytes 49160 | tf_op jit(solution)/shard_map/ppermute | solution.py:14
  330.6 13.3 %collective-permute-start.12 = (f32[32,128]{1,0:T(8,128)S(1)}, f32[32,128]{1,0:T(8,128)S(1)}, u32[]{:S(2)}, u32[]{:S(2)}) collective-permute-start(f32[32,128]{1,0:T(8,128)S(1)} %get-tuple-element.32), channel_id=1, source_target_pairs={{0,16},{16,32},{32,48},{48,64},{64,80},{80,96},{96,112},{112,128},... | collective-permute-start | bytes 49160 | tf_op jit(solution)/shard_map/ppermute | solution.py:14
  366.5 5.5 %collective-permute-start.13 = (f32[32,512]{1,0:T(8,128)S(1)}, f32[32,512]{1,0:T(8,128)S(1)}, u32[]{:S(2)}, u32[]{:S(2)}) collective-permute-start(f32[32,512]{1,0:T(8,128)S(1)} %get-tuple-element.10), channel_id=1, source_target_pairs={{0,496},{16,0},{32,16},{48,32},{64,48},{80,64},{96,80},{112,96},{1... | collective-permute-start | bytes 196616 | tf_op jit(solution)/shard_map/ppermute | solution.py:14
  368.5 13.7 %collective-permute-start.14 = (f32[32,512]{1,0:T(8,128)S(1)}, f32[32,512]{1,0:T(8,128)S(1)}, u32[]{:S(2)}, u32[]{:S(2)}) collective-permute-start(f32[32,512]{1,0:T(8,128)S(1)} %get-tuple-element.11), channel_id=1, source_target_pairs={{0,16},{16,32},{32,48},{48,64},{64,80},{80,96},{96,112},{112,128},... | collective-permute-start | bytes 196616 | tf_op jit(solution)/shard_map/ppermute | solution.py:14
  438.2 6.7 %collective-permute-start.15 = (f32[32,128]{1,0:T(8,128)S(1)}, f32[32,128]{1,0:T(8,128)S(1)}, u32[]{:S(2)}, u32[]{:S(2)}) collective-permute-start(f32[32,128]{1,0:T(8,128)S(1)} %get-tuple-element.27), channel_id=1, source_target_pairs={{0,496},{16,0},{32,16},{48,32},{64,48},{80,64},{96,80},{112,96},{1... | collective-permute-start | bytes 49160 | tf_op jit(solution)/shard_map/ppermute | solution.py:14
  440.1 13.2 %collective-permute-start.16 = (f32[32,128]{1,0:T(8,128)S(1)}, f32[32,128]{1,0:T(8,128)S(1)}, u32[]{:S(2)}, u32[]{:S(2)}) collective-permute-start(f32[32,128]{1,0:T(8,128)S(1)} %get-tuple-element.28), channel_id=1, source_target_pairs={{0,16},{16,32},{32,48},{48,64},{64,80},{80,96},{96,112},{112,128},... | collective-permute-start | bytes 49160 | tf_op jit(solution)/shard_map/ppermute | solution.py:14
  454.7 21.9 %all-to-all-start.11 = ((bf16[16,2,32,128]{3,2,1,0:T(8,128)(2,1)}), bf16[16,2,32,128]{3,2,1,0:T(8,128)(2,1)S(1)}, u32[]{:S(2)}, u32[]{:S(2)}) async-start(bf16[16,2,32,128]{3,2,1,0:T(8,128)(2,1)} %broadcast_in_dim.29), calls=%async_computation.11 | async-start | bytes 524288 | tf_op jit(solution)/shard_map/all_to_all | solution.py:19
where the time goes:
time: 480 us; the launch traced here: 479 us
  blocking collectives  214 us (45%)
  waiting for transfers between devices  128 us (27%)
  starting transfers between devices  68.8 us (14%)
  other arithmetic  50.9 us (11%)
  matrix products  10.9 us (2%)
    all_to_all x6, blocking collectives, sent_to_all(): lax.all_to_all(jnp.broadcast_to(value[None], (peers, *value.shape)), axis...  135 us
    ppermute x17, waiting for transfers between devices, passed_along(): lax.ppermute(value, axis, [(i, (i + by) % peers) for i in range(peers)])  97.6 us
    all_to_all x4, blocking collectives, summed_on_arrival(): lax.all_to_all(pieces, axis, split_axis=0, concat_axis=0, tiled=True)  78.7 us
    ppermute x17, starting transfers between devices, passed_along(): lax.ppermute(value, axis, [(i, (i + by) % peers) for i in range(peers)])  47.3 us
    all_to_all x2, waiting for transfers between devices, sent_to_all(): lax.all_to_all(jnp.broadcast_to(value[None], (peers, *value.shape)), axis...  30.7 us
    another operation x13, other arithmetic, on_device(): lower_factor = jnp.linalg.cholesky(gram)  24.1 us
    all_to_all x2, starting transfers between devices, sent_to_all(): lax.all_to_all(jnp.broadcast_to(value[None], (peers, *value.shape)), axis...  21.5 us
    another operation x9, other arithmetic, lower_solve(): jax.scipy.linalg.solve_triangular(lower_factor, right_hand, lower=True)  20 us
  transfers between devices with their start and end apart: 19, of which 13 were waited for; matrix products, arithmetic and copies ran while one was open for 0% of the time, Pallas kernels for 0%

commit v1 on v0

v1 whole, which is shorter than its diff:
```python
import jax
import jax.numpy as jnp
from jax import lax
from jax.experimental import pallas as pl
from jax.experimental.pallas import tpu as pltpu
from jax.sharding import PartitionSpec as P

POWER = 4
MIXING = 1.0 / 3.0
MESH = pl.DeviceIdType.MESH
HIGHEST = lax.Precision.HIGHEST
F32 = jnp.float32
BF16 = jnp.bfloat16

RANK = 32
RING = 8
ROWS = 512
WID = 2048
LANES = 128
CHUNKS = 4
CHUNK_ROWS = ROWS // CHUNKS


def mix(a, b, dims):
    return lax.dot_general(a, b, (dims, ((), ())), preferred_element_type=F32)


def mix_exact(a, b, dims):
    return lax.dot_general(
        a, b, (dims, ((), ())), precision=HIGHEST, preferred_element_type=F32
    )


def inverse_lower(packed):
    lane = lax.broadcasted_iota(jnp.int32, (8, LANES), 1)
    row = lax.broadcasted_iota(jnp.int32, (8, LANES), 0)
    parts = []
    for j in range(4):
        shift = (RANK - RANK * j) % LANES
        moved = packed if shift == 0 else pltpu.roll(packed, shift, 1)
        unit = (lane == row + 8 * j).astype(F32)
        parts.append(jnp.where(lane < RANK, unit, jnp.where(lane < 2 * RANK, moved, 0.0)))
    for k in range(RANK):
        own = k // 8
        pivot_row = parts[own][k % 8 : k % 8 + 1, :]
        columns = {}
        for i in range(own, 4):
            columns[i] = jnp.broadcast_to(parts[i][:, RANK + k : RANK + k + 1], (8, LANES))
        pivot = columns[own][k % 8 : k % 8 + 1, :]
        scaled = pivot_row / pivot
        for i in range(own, 4):
            column = columns[i]
            if i == own:
                column = jnp.where(row > k % 8, column, 0.0)
            parts[i] = parts[i] - column * scaled
    done = []
    for j in range(4):
        diagonal = jnp.sum(
            jnp.where(lane == row + RANK + 8 * j, parts[j], 0.0), axis=1, keepdims=True
        )
        done.append(jnp.where(lane < RANK, parts[j] / jnp.sqrt(diagonal), 0.0))
    return jnp.concatenate(done, axis=0)


def kernel(
    w_hbm,
    warm_ref,
    signed_ref,
    pair_ref,
    new_ref,
    wbuf,
    wside,
    fbuf,
    fprior,
    bprior,
    raw,
    halves,
    partial,
    arrived,
    gram_own,
    gram_all,
    gram_plane,
    gram_far,
    plane,
    far,
    summed,
    basis,
    w_sem,
    ws_sem,
    wr_sem,
    gs_sem,
    gr_sem,
    ps_sem,
    pr_sem,
    zs_sem,
    zr_sem,
    zgs_sem,
    zgr_sem,
    fs_sem,
    fr_sem,
    es_sem,
    er_sem,
    bs_sem,
    br_sem,
    hs_sem,
    hr_sem,
):
    blk = lax.axis_index("blk")
    shard = lax.axis_index("shard")
    blks = lax.axis_size("blk")
    x = shard // 4
    far_half = lax.rem(shard // 2, 2)
    core = lax.rem(shard, 2)
    place = 2 * x + core
    above = lax.rem(blk + 1, blks)
    below = lax.rem(blk + blks - 1, blks)
    across = 4 * x + 2 * (1 - far_half) + core
    turns_up = lax.rem(blk, RING) // (RING - 1)
    turns_down = (RING - 1 - lax.rem(blk, RING)) // (RING - 1)
    half_up = lax.rem(far_half + turns_up, 2)
    half_down = lax.rem(far_half + turns_down, 2)
    shard_up = 4 * x + 2 * half_up + core
    shard_down = 4 * x + 2 * half_down + core

    def mate(dx, dc):
        return 4 * lax.rem(x + dx, 4) + 2 * far_half + lax.rem(core + dc, 2)


    others = [(dx, dc) for dx in (2, 1, 3, 0) for dc in (0, 1) if dx or dc]

    def remote(src, dst, send, recv, to_blk, to_shard):
        return pltpu.make_async_remote_copy(
            src_ref=src,
            dst_ref=dst,
            send_sem=send,
            recv_sem=recv,
            device_id=(to_blk, to_shard),
            device_id_type=MESH,
        )

    barrier = pltpu.get_barrier_semaphore()
    greeted = [(below, shard), (above, shard), (blk, across), (above, shard_up), (below, shard_down)]
    greeted += [(blk, mate(dx, dc)) for dx, dc in others]
    for peer in greeted:
        pl.semaphore_signal(barrier, inc=1, device_id=peer, device_id_type=MESH)
    load = pltpu.make_async_copy(w_hbm, wbuf.at[pl.ds(0, ROWS), :], w_sem)
    load.start()
    for q in range(16):
        fbuf[q] = warm_ref[:, q * LANES : (q + 1) * LANES].astype(BF16)
    raw[...] = jnp.zeros_like(raw)
    summed[...] = jnp.zeros_like(summed)
    pl.semaphore_wait(barrier, len(greeted))

    def weight_copy(c):
        rows = pl.ds(c * CHUNK_ROWS, CHUNK_ROWS)
        return remote(
            w_hbm.at[rows, :],
            wbuf.at[pl.ds(ROWS + c * CHUNK_ROWS, CHUNK_ROWS), :],
            ws_sem.at[c],
            wr_sem.at[c],
            below,
            shard,
        )

    for c in range(CHUNKS):
        weight_copy(c).start()
    load.wait()

    def turn(c):
        start = c * CHUNK_ROWS
        for q in range(16):
            wside[q * LANES : (q + 1) * LANES, start : start + CHUNK_ROWS] = wbuf[
                start : start + CHUNK_ROWS, q * LANES : (q + 1) * LANES
            ].T

    for c in range(CHUNKS):
        turn(c)
    for c in range(CHUNKS):
        weight_copy(c).wait_recv()
        turn(CHUNKS + c)
    for c in range(CHUNKS):
        weight_copy(c).wait_send()

    lane8 = lax.broadcasted_iota(jnp.int32, (8, LANES), 1) // RANK

    def gram_copy(dx, dc):
        t = 2 * dx + dc
        return remote(
            gram_own, gram_all.at[place], gs_sem.at[t], gr_sem.at[t], blk, mate(dx, dc)
        )

    def part_copy(j, dx, dc):
        t = 2 * dx + dc
        return remote(
            partial.at[j, t], arrived.at[j, t], ps_sem.at[j, t], pr_sem.at[j, t], blk, mate(dx, dc)
        )

    def gather_copy(j, dx, dc):
        t = 2 * dx + dc
        q = 4 * x + 2 * j + core
        return remote(
            fbuf.at[q], fbuf.at[q], fs_sem.at[j, t], fr_sem.at[j, t], blk, mate(dx, dc)
        )

    def far_gram_copy(slot):
        return remote(gram_plane.at[slot], gram_far.at[slot], zgs_sem.at[slot], zgr_sem.at[slot], blk, across)

    def far_copy(slot, j):
        return remote(plane.at[slot, j], far.at[slot, j], zs_sem.at[slot, j], zr_sem.at[slot, j], blk, across)

    def up_copy(j):
        q = 4 * x + 2 * j + core
        return remote(fbuf.at[q], fprior.at[q], es_sem.at[j], er_sem.at[j], above, shard_up)

    def pass_copy(j, dx, dc):
        t = 2 * dx + dc
        q = 4 * x + 2 * j + core
        return remote(
            fprior.at[q], fprior.at[q], hs_sem.at[j, t], hr_sem.at[j, t], blk, mate(dx, dc)
        )

    basis_copy = remote(basis, bprior, bs_sem, br_sem, above, shard)

    def step(k, carry):
        slot = lax.rem(k, 2)
        factor = jnp.concatenate([fbuf[q] for q in range(16)], axis=1)
        own = mix(factor, wside[...], ((1,), (0,)))
        raw_now = own[:, :ROWS] - own[:, ROWS:]
        raw[0:RANK, :] = raw_now
        stacked = jnp.concatenate([raw_now] * 4, axis=0)
        gram4 = mix_exact(raw_now, stacked, ((1,), (1,)))
        packed = gram4[0:8]
        for j in range(1, 4):
            packed = jnp.where(lane8 == j, gram4[8 * j : 8 * j + 8], packed)
        gram_own[...] = packed
        gram_all[place] = packed
        for dx, dc in others:
            gram_copy(dx, dc).start()
        high = raw_now.astype(BF16)
        low = (raw_now - high.astype(F32)).astype(BF16)
        halves[0:RANK, :ROWS] = high
        halves[0:RANK, ROWS:] = -high
        halves[RANK:, :ROWS] = low
        halves[RANK:, ROWS:] = -low

        for j in range(2):
            for dx in (2, 1, 3, 0):
                start = pl.multiple_of(512 * lax.rem(x + dx, 4) + 256 * j, 256)
                both = mix(halves[...], wbuf[:, pl.ds(start, 256)], ((1,), (0,)))
                piece = both[:RANK] + both[RANK:]
                first = 2 * dx + core
                second = 2 * dx + 1 - core
                if dx:
                    partial[j, first] = piece[:, :LANES]
                    partial[j, second] = piece[:, LANES:]
                    part_copy(j, dx, 0).start()
                    part_copy(j, dx, 1).start()
                else:
                    partial[j, first] = piece[:, :LANES]
                    partial[j, second] = piece[:, LANES:]
                    part_copy(j, 0, 1).start()
            if j == 0:
                for dx, dc in others:
                    gram_copy(dx, dc).wait_recv()
                gram_plane[slot] = jnp.sum(gram_all[...], axis=0)
                far_gram_copy(slot).start()
        for j in range(2):
            total = partial[j, 0]
            for dx, dc in others:
                part_copy(j, dx, dc).wait_recv()
            for t in range(1, 8):
                total = total + arrived[j, t]
            plane[slot, j] = total
            far_copy(slot, j).start()
        far_gram_copy(slot).wait_recv()
        lower_inv = inverse_lower(gram_plane[slot] + gram_far[slot])

        @pl.when(k == POWER - 1)
        def _():
            basis[...] = mix_exact(lower_inv, raw[...], ((1,), (0,))).astype(BF16)
            basis_copy.start()

        for dx, dc in others:
            for j in range(2):
                part_copy(j, dx, dc).wait_send()
        for j in range(2):
            far_copy(slot, j).wait_recv()
            summed[0:RANK, :] = plane[slot, j] + far[slot, j]
            piece = mix_exact(lower_inv, summed[...], ((1,), (0,)))
            fbuf[4 * x + 2 * j + core] = piece.astype(BF16)

            @pl.when(k == POWER - 1)
            def _():
                @pl.when(far_half == j)
                def _():
                    new_ref[...] = piece

                up_copy(j).start()

            for dx, dc in others:
                gather_copy(j, dx, dc).start()
        for dx, dc in others:
            gram_copy(dx, dc).wait_send()
        far_gram_copy(slot).wait_send()
        for j in range(2):
            far_copy(slot, j).wait_send()
        for j in range(2):
            for dx, dc in others:
                gather_copy(j, dx, dc).wait()
        return carry

    lax.fori_loop(0, POWER, step, 0)

    for j in range(2):
        up_copy(j).wait_recv()
        for dx, dc in others:
            pass_copy(j, dx, dc).start()
    for q in range(16):
        pair_ref[RANK:, q * LANES : (q + 1) * LANES] = fbuf[q]
    signed_ref[RANK:, :] = -basis[...]
    basis_copy.wait_recv()
    signed_ref[0:RANK, :] = bprior[...]
    for j in range(2):
        for dx, dc in others:
            pass_copy(j, dx, dc).wait()
    for q in range(16):
        pair_ref[0:RANK, q * LANES : (q + 1) * LANES] = fprior[q]
    basis_copy.wait_send()
    for j in range(2):
        up_copy(j).wait_send()


def on_device(weights, warm_factor):
    local_weight = weights[0]
    vmem = pl.BlockSpec(memory_space=pltpu.VMEM)
    dma = pltpu.SemaphoreType.DMA
    signed, factor_pair, new_factor = pl.pallas_call(
        kernel,
        out_shape=(
            jax.ShapeDtypeStruct((2 * RANK, ROWS), BF16),
            jax.ShapeDtypeStruct((2 * RANK, WID), BF16),
            jax.ShapeDtypeStruct((RANK, LANES), F32),
        ),
        in_specs=[pl.BlockSpec(memory_space=pl.ANY), vmem],
        out_specs=(vmem, vmem, vmem),
        scratch_shapes=[
            pltpu.VMEM((2 * ROWS, WID), BF16),
            pltpu.VMEM((WID, 2 * ROWS), BF16),
            pltpu.VMEM((16, RANK, LANES), BF16),
            pltpu.VMEM((16, RANK, LANES), BF16),
            pltpu.VMEM((RANK, ROWS), BF16),
            pltpu.VMEM((LANES, ROWS), F32),
            pltpu.VMEM((2 * RANK, 2 * ROWS), BF16),
            pltpu.VMEM((2, 8, RANK, LANES), F32),
            pltpu.VMEM((2, 8, RANK, LANES), F32),
            pltpu.VMEM((8, LANES), F32),
            pltpu.VMEM((8, 8, LANES), F32),
            pltpu.VMEM((2, 8, LANES), F32),
            pltpu.VMEM((2, 8, LANES), F32),
            pltpu.VMEM((2, 2, RANK, LANES), F32),
            pltpu.VMEM((2, 2, RANK, LANES), F32),
            pltpu.VMEM((LANES, LANES), F32),
            pltpu.VMEM((RANK, ROWS), BF16),
            dma,
            dma((CHUNKS,)),
            dma((CHUNKS,)),
            dma((8,)),
            dma((8,)),
            dma((2, 8)),
            dma((2, 8)),
            dma((2, 2)),
            dma((2, 2)),
            dma((2,)),
            dma((2,)),
            dma((2, 8)),
            dma((2, 8)),
            dma((2,)),
            dma((2,)),
            dma,
            dma,
            dma((2, 8)),
            dma((2, 8)),
        ],
        compiler_params=pltpu.CompilerParams(collective_id=0, has_side_effects=True),
        name="power_rounds",
    )(local_weight, warm_factor[0])
    delta = jnp.einsum("jr,jc->rc", signed, factor_pair, preferred_element_type=F32)
    new_weight = (local_weight.astype(F32) + MIXING * delta).astype(BF16)
    return (new_weight[None], new_factor[None])


def solution(mesh):
    return jax.shard_map(
        on_device,
        mesh=mesh,
        in_specs=(P("blk", "shard", None), P("blk", None, None)),
        out_specs=(P("blk", "shard", None), P("blk", None, "shard")),
        check_vma=False,
    )
```

time: 480 us -> 160 us (0.33)
  blocking collectives: 214 us -> 0 us
  Pallas kernels: 0 us -> 155 us
  waiting for transfers between devices: 128 us -> 0 us
  starting transfers between devices: 68.8 us -> 0 us
  other arithmetic: 50.9 us -> 0 us
  matrix products: 10.9 us -> 3.04 us
    all_to_all x10 -> x0, blocking collectives: 214 us -> none  [the longest x6 135 us: sent_to_all(): lax.all_to_all(jnp.broadcast_to(value[None], (peers, *value.shape)), axis...]
    pallas_call x0 -> x1, Pallas kernels: none -> 155 us  [on_device(): pl.pallas_call(kernel, out_shape=(jax.ShapeDtypeStruct((2 * RANK, ROWS),...]
    ppermute x17 -> x0, waiting for transfers between devices: 97.6 us -> none  [passed_along(): lax.ppermute(value, axis, [(i, (i + by) % peers) for i in range(peers)])]
    ppermute x17 -> x0, starting transfers between devices: 47.3 us -> none  [passed_along(): lax.ppermute(value, axis, [(i, (i + by) % peers) for i in range(peers)])]
    another operation x34 -> x0, other arithmetic: 44.8 us -> none  [the longest x13 24.1 us: on_device(): lower_factor = jnp.linalg.cholesky(gram)]
    all_to_all x2 -> x0, waiting for transfers between devices: 30.7 us -> none  [sent_to_all(): lax.all_to_all(jnp.broadcast_to(value[None], (peers, *value.shape)), axis...]
    all_to_all x2 -> x0, starting transfers between devices: 21.5 us -> none  [sent_to_all(): lax.all_to_all(jnp.broadcast_to(value[None], (peers, *value.shape)), axis...]
    dot_general x13 -> x1, matrix products: 9.57 us -> 3.04 us  [on_device(): jnp.einsum('jr,jc->rc', signed, factor_pair, preferred_element_type=F32)]
  transfers between devices with their start and end apart: 19 -> 0, of which waited for: 13 -> 0; matrix products, arithmetic and copies ran while one was open for 0% -> 0% of each run, Pallas kernels for 0% -> 0%
where the time goes in v1:
time: 160 us
  Pallas kernels  155 us (97%)
  matrix products  3.04 us (2%)
    pallas_call x1, Pallas kernels, on_device(): pl.pallas_call(kernel, out_shape=(jax.ShapeDtypeStruct((2 * RANK, ROWS),...  155 us

profile of v1, /device:TPU:1, one launch (start us, length us, event | category | flops | bytes accessed | tf_op | source)
XLA Modules:
  0.0 159.5 jit_solution(13797424848053683649)
XLA Ops:
  0.6 0.0 copy-start
  0.6 155.2 %power_rounds.1 = (bf16[64,512]{1,0:T(8,128)(2,1)}, bf16[64,2048]{1,0:T(8,128)(2,1)}, f32[32,128]{1,0:T(8,128)}) custom-call(bf16[512,2048]{1,0:T(8,128)(2,1)} %bitcast.8, f32[32,2048]{1,0:T(8,128)} %bitcast.9), custom_call_target="tpu_custom_call" | custom-call | tf_op jit(solution)/shard_map/power_rounds/pallas_call | solution.py:337
  155.9 0.0 copy-done
  155.9 0.0 copy-start.1
  155.9 3.0 %fusion = bf16[1,512,2048]{2,1,0:T(8,128)(2,1)} fusion(bf16[64,512]{1,0:T(8,128)(2,1)} %get-tuple-element.5, bf16[64,2048]{1,0:T(8,128)(2,1)} %get-tuple-element.6, bf16[1,512,2048]{2,1,0:T(8,128)(2,1)S(1)} %copy-done), kind=kOutput, calls=%fused_computation.1 | convolution fusion | flops 138412032 | bytes 4521984 | tf_op jit(solution)/shard_map/jr,jc->rc/dot_general | solution.py:387
  158.9 0.0 copy-done.1
  158.9 0.6 copy.5
Async XLA Ops:
  0.6 155.2 %copy-start = (bf16[1,512,2048]{2,1,0:T(8,128)(2,1)S(1)}, bf16[1,512,2048]{2,1,0:T(8,128)(2,1)}, u32[]{:S(2)}) copy-start(bf16[1,512,2048]{2,1,0:T(8,128)(2,1)} %param.2) | copy-start | bytes 6291460
  155.9 3.1 %copy-start.1 = (f32[32,128]{1,0:T(8,128)S(1)}, f32[32,128]{1,0:T(8,128)}, u32[]{:S(2)}) copy-start(f32[32,128]{1,0:T(8,128)} %get-tuple-element.7) | copy-start | bytes 49156

commit v2 on v1

--- a/solution.py
+++ b/solution.py
@@ -19,6 +19,7 @@
 LANES = 128
 CHUNKS = 4
 CHUNK_ROWS = ROWS // CHUNKS
+BLOCK = 4
 
 
 def mix(a, b, dims):
@@ -40,19 +41,30 @@
         moved = packed if shift == 0 else pltpu.roll(packed, shift, 1)
         unit = (lane == row + 8 * j).astype(F32)
         parts.append(jnp.where(lane < RANK, unit, jnp.where(lane < 2 * RANK, moved, 0.0)))
-    for k in range(RANK):
-        own = k // 8
-        pivot_row = parts[own][k % 8 : k % 8 + 1, :]
-        columns = {}
-        for i in range(own, 4):
-            columns[i] = jnp.broadcast_to(parts[i][:, RANK + k : RANK + k + 1], (8, LANES))
-        pivot = columns[own][k % 8 : k % 8 + 1, :]
-        scaled = pivot_row / pivot
-        for i in range(own, 4):
-            column = columns[i]
-            if i == own:
-                column = jnp.where(row > k % 8, column, 0.0)
-            parts[i] = parts[i] - column * scaled
+    for k in range(0, RANK, BLOCK):
+        own, top = k // 8, k % 8
+        columns = [
+            [
+                jnp.broadcast_to(parts[i][:, RANK + k + c : RANK + k + c + 1], (8, LANES))
+                for i in range(own, 4)
+            ]
+            for c in range(BLOCK)
+        ]
+        rows = [parts[own][top + c : top + c + 1, :] for c in range(BLOCK)]
+        for c in range(BLOCK):
+            head = columns[c][0]
+            inverse = 1.0 / head[top + c : top + c + 1, :]
+            scaled = rows[c] * inverse
+            for d in range(c + 1, BLOCK):
+                entry = head[top + d : top + d + 1, :]
+                ratio = entry * inverse
+                rows[d] = rows[d] - entry * scaled
+                columns[d] = [u - v * ratio for u, v in zip(columns[d], columns[c])]
+            for i in range(own, 4):
+                column = columns[c][i - own]
+                if i == own:
+                    column = jnp.where(row > top + c, column, 0.0)
+                parts[i] = parts[i] - column * scaled
     done = []
     for j in range(4):
         diagonal = jnp.sum(
@@ -125,7 +137,6 @@
     def mate(dx, dc):
         return 4 * lax.rem(x + dx, 4) + 2 * far_half + lax.rem(core + dc, 2)
 
-
     others = [(dx, dc) for dx in (2, 1, 3, 0) for dc in (0, 1) if dx or dc]
 
     def remote(src, dst, send, recv, to_blk, to_shard):
@@ -143,8 +154,16 @@
     greeted += [(blk, mate(dx, dc)) for dx, dc in others]
     for peer in greeted:
         pl.semaphore_signal(barrier, inc=1, device_id=peer, device_id_type=MESH)
-    load = pltpu.make_async_copy(w_hbm, wbuf.at[pl.ds(0, ROWS), :], w_sem)
-    load.start()
+
+    def load(c):
+        return pltpu.make_async_copy(
+            w_hbm.at[pl.ds(c * CHUNK_ROWS, CHUNK_ROWS), :],
+            wbuf.at[pl.ds(2 * c * CHUNK_ROWS, CHUNK_ROWS), :],
+            w_sem.at[c],
+        )
+
+    for c in range(CHUNKS):
+        load(c).start()
     for q in range(16):
         fbuf[q] = warm_ref[:, q * LANES : (q + 1) * LANES].astype(BF16)
     raw[...] = jnp.zeros_like(raw)
@@ -155,7 +174,7 @@
         rows = pl.ds(c * CHUNK_ROWS, CHUNK_ROWS)
         return remote(
             w_hbm.at[rows, :],
-            wbuf.at[pl.ds(ROWS + c * CHUNK_ROWS, CHUNK_ROWS), :],
+            wbuf.at[pl.ds((2 * c + 1) * CHUNK_ROWS, CHUNK_ROWS), :],
             ws_sem.at[c],
             wr_sem.at[c],
             below,
@@ -164,22 +183,18 @@
 
     for c in range(CHUNKS):
         weight_copy(c).start()
-    load.wait()
-
-    def turn(c):
-        start = c * CHUNK_ROWS
+
+    def turn(part):
+        start = pl.multiple_of(part * CHUNK_ROWS, CHUNK_ROWS)
         for q in range(16):
-            wside[q * LANES : (q + 1) * LANES, start : start + CHUNK_ROWS] = wbuf[
-                start : start + CHUNK_ROWS, q * LANES : (q + 1) * LANES
+            wside[q * LANES : (q + 1) * LANES, pl.ds(start, CHUNK_ROWS)] = wbuf[
+                pl.ds(start, CHUNK_ROWS), q * LANES : (q + 1) * LANES
             ].T
 
+    partial[...] = jnp.zeros_like(partial)
     for c in range(CHUNKS):
-        turn(c)
-    for c in range(CHUNKS):
-        weight_copy(c).wait_recv()
-        turn(CHUNKS + c)
-    for c in range(CHUNKS):
-        weight_copy(c).wait_send()
+        load(c).wait()
+        turn(2 * c)
 
     lane8 = lax.broadcasted_iota(jnp.int32, (8, LANES), 1) // RANK
 
@@ -221,12 +236,8 @@
 
     basis_copy = remote(basis, bprior, bs_sem, br_sem, above, shard)
 
-    def step(k, carry):
-        slot = lax.rem(k, 2)
-        factor = jnp.concatenate([fbuf[q] for q in range(16)], axis=1)
-        own = mix(factor, wside[...], ((1,), (0,)))
-        raw_now = own[:, :ROWS] - own[:, ROWS:]
-        raw[0:RANK, :] = raw_now
+    def send_gram():
+        raw_now = raw[0:RANK, :]
         stacked = jnp.concatenate([raw_now] * 4, axis=0)
         gram4 = mix_exact(raw_now, stacked, ((1,), (1,)))
         packed = gram4[0:8]
@@ -236,34 +247,78 @@
         gram_all[place] = packed
         for dx, dc in others:
             gram_copy(dx, dc).start()
-        high = raw_now.astype(BF16)
-        low = (raw_now - high.astype(F32)).astype(BF16)
-        halves[0:RANK, :ROWS] = high
-        halves[0:RANK, ROWS:] = -high
-        halves[RANK:, :ROWS] = low
-        halves[RANK:, ROWS:] = -low
-
+
+    def keep_halves(value, start):
+        high = value.astype(BF16)
+        low = (value - high.astype(F32)).astype(BF16)
+        here, there = pl.ds(start, CHUNK_ROWS), pl.ds(start + CHUNK_ROWS, CHUNK_ROWS)
+        halves[0:RANK, here] = high
+        halves[0:RANK, there] = -high
+        halves[RANK:, here] = low
+        halves[RANK:, there] = -low
+
+    def product(rows, j, dx):
+        start = pl.multiple_of(512 * lax.rem(x + dx, 4) + 256 * j, 256)
+        both = mix(halves[:, rows], wbuf[rows, pl.ds(start, 256)], ((1,), (0,)))
+        piece = both[:RANK] + both[RANK:]
+        return (2 * dx + core, piece[:, :LANES]), (2 * dx + 1 - core, piece[:, LANES:])
+
+    def send_parts(j, dx):
+        for dc in (0, 1):
+            if dx or dc:
+                part_copy(j, dx, dc).start()
+
+    order = [(j, dx) for j in range(2) for dx in (2, 1, 3, 0)]
+
+    first_factor = jnp.concatenate([fbuf[q] for q in range(16)], axis=1)
+
+    def first_chunk(c, carry):
+        weight_copy(c).wait_recv()
+        turn(2 * c + 1)
+        start = pl.multiple_of(2 * CHUNK_ROWS * c, 2 * CHUNK_ROWS)
+        rows = pl.ds(start, 2 * CHUNK_ROWS)
+        own = mix(first_factor, wside[:, rows], ((1,), (0,)))
+        value = own[:, :CHUNK_ROWS] - own[:, CHUNK_ROWS:]
+        raw[0:RANK, pl.ds(pl.multiple_of(CHUNK_ROWS * c, CHUNK_ROWS), CHUNK_ROWS)] = value
+        keep_halves(value, start)
+        for j, dx in order:
+            for t, piece in product(rows, j, dx):
+                partial[j, t] = partial[j, t] + piece
+        return carry
+
+    lax.fori_loop(0, CHUNKS, first_chunk, 0)
+    for j, dx in order:
+        send_parts(j, dx)
+    send_gram()
+    for c in range(CHUNKS):
+        weight_copy(c).wait_send()
+
+    def forward():
+        own = jnp.zeros((RANK, 2 * ROWS), F32)
         for j in range(2):
-            for dx in (2, 1, 3, 0):
-                start = pl.multiple_of(512 * lax.rem(x + dx, 4) + 256 * j, 256)
-                both = mix(halves[...], wbuf[:, pl.ds(start, 256)], ((1,), (0,)))
-                piece = both[:RANK] + both[RANK:]
-                first = 2 * dx + core
-                second = 2 * dx + 1 - core
-                if dx:
-                    partial[j, first] = piece[:, :LANES]
-                    partial[j, second] = piece[:, LANES:]
-                    part_copy(j, dx, 0).start()
-                    part_copy(j, dx, 1).start()
-                else:
-                    partial[j, first] = piece[:, :LANES]
-                    partial[j, second] = piece[:, LANES:]
-                    part_copy(j, 0, 1).start()
-            if j == 0:
-                for dx, dc in others:
-                    gram_copy(dx, dc).wait_recv()
-                gram_plane[slot] = jnp.sum(gram_all[...], axis=0)
-                far_gram_copy(slot).start()
+            for dx, dc in others:
+                gather_copy(j, dx, dc).wait()
+            for q in range(2 * j, 16, 4):
+                factor = jnp.concatenate([fbuf[q], fbuf[q + 1]], axis=1)
+                own = own + mix(factor, wside[q * LANES : (q + 2) * LANES, :], ((1,), (0,)))
+        for c in range(CHUNKS):
+            start = 2 * CHUNK_ROWS * c
+            middle, end = start + CHUNK_ROWS, start + 2 * CHUNK_ROWS
+            value = own[:, start:middle] - own[:, middle:end]
+            raw[0:RANK, CHUNK_ROWS * c : CHUNK_ROWS * (c + 1)] = value
+            keep_halves(value, start)
+        send_gram()
+        for j, dx in order:
+            for t, piece in product(slice(None), j, dx):
+                partial[j, t] = piece
+            send_parts(j, dx)
+
+    def step(k, carry):
+        slot = lax.rem(k, 2)
+        for dx, dc in others:
+            gram_copy(dx, dc).wait_recv()
+        gram_plane[slot] = jnp.sum(gram_all[...], axis=0)
+        far_gram_copy(slot).start()
         for j in range(2):
             total = partial[j, 0]
             for dx, dc in others:
@@ -304,13 +359,14 @@
         far_gram_copy(slot).wait_send()
         for j in range(2):
             far_copy(slot, j).wait_send()
-        for j in range(2):
-            for dx, dc in others:
-                gather_copy(j, dx, dc).wait()
+        pl.when(k < POWER - 1)(forward)
         return carry
 
     lax.fori_loop(0, POWER, step, 0)
 
+    for j in range(2):
+        for dx, dc in others:
+            gather_copy(j, dx, dc).wait()
     for j in range(2):
         up_copy(j).wait_recv()
         for dx, dc in others:
@@ -328,6 +384,12 @@
     basis_copy.wait_send()
     for j in range(2):
         up_copy(j).wait_send()
+
+
+def update_kernel(signed_ref, pair_ref, w_ref, factor_ref, out_ref, new_ref):
+    delta = mix(signed_ref[...], pair_ref[...], ((0,), (0,)))
+    out_ref[0] = (w_ref[...].astype(F32) + MIXING * delta).astype(BF16)
+    new_ref[0] = factor_ref[...]
 
 
 def on_device(weights, warm_factor):
@@ -361,7 +423,7 @@
             pltpu.VMEM((2, 2, RANK, LANES), F32),
             pltpu.VMEM((LANES, LANES), F32),
             pltpu.VMEM((RANK, ROWS), BF16),
-            dma,
+            dma((CHUNKS,)),
             dma((CHUNKS,)),
             dma((CHUNKS,)),
             dma((8,)),
@@ -384,9 +446,27 @@
         compiler_params=pltpu.CompilerParams(collective_id=0, has_side_effects=True),
         name="power_rounds",
     )(local_weight, warm_factor[0])
-    delta = jnp.einsum("jr,jc->rc", signed, factor_pair, preferred_element_type=F32)
-    new_weight = (local_weight.astype(F32) + MIXING * delta).astype(BF16)
-    return (new_weight[None], new_factor[None])
+    columns = 512
+    new_weight, new_factor = pl.pallas_call(
+        update_kernel,
+        grid=(WID // columns,),
+        out_shape=(
+            jax.ShapeDtypeStruct((1, ROWS, WID), BF16),
+            jax.ShapeDtypeStruct((1, RANK, LANES), F32),
+        ),
+        in_specs=[
+            pl.BlockSpec((2 * RANK, ROWS), lambda i: (0, 0)),
+            pl.BlockSpec((2 * RANK, columns), lambda i: (0, i)),
+            pl.BlockSpec((ROWS, columns), lambda i: (0, i)),
+            pl.BlockSpec((RANK, LANES), lambda i: (0, 0)),
+        ],
+        out_specs=(
+            pl.BlockSpec((1, ROWS, columns), lambda i: (0, 0, i)),
+            pl.BlockSpec((1, RANK, LANES), lambda i: (0, 0, 0)),
+        ),
+        name="update",
+    )(signed, factor_pair, local_weight, new_factor)
+    return new_weight, new_factor
 
 
 def solution(mesh):

time: 160 us -> 152 us (0.950)
  Pallas kernels: 155 us -> 151 us
  matrix products: 3.04 us -> 0 us
    pallas_call x1, Pallas kernels: 155 us -> 147 us  [on_device(): pl.pallas_call(kernel, out_shape=(jax.ShapeDtypeStruct((2 * RANK, ROWS),...]
    pallas_call x0 -> x1, Pallas kernels: none -> 4.44 us  [on_device(): pl.pallas_call(update_kernel, grid=(WID // columns,), out_shape=(jax.Shap...]
    dot_general x1 -> x0, matrix products: 3.04 us -> none  [on_device(): jnp.einsum('jr,jc->rc', signed, factor_pair, preferred_element_type=F32)]
where the time goes in v2:
time: 152 us
  Pallas kernels  151 us (99%)
    pallas_call x1, Pallas kernels, on_device(): pl.pallas_call(kernel, out_shape=(jax.ShapeDtypeStruct((2 * RANK, ROWS),...  147 us
    pallas_call x1, Pallas kernels, on_device(): pl.pallas_call(update_kernel, grid=(WID // columns,), out_shape=(jax.Shap...  4.44 us

profile of v2, /device:TPU:1, one launch (start us, length us, event | category | flops | bytes accessed | tf_op | source)
XLA Modules:
  0.0 151.9 jit_solution(4797587334093977132)
XLA Ops:
  0.6 146.8 %power_rounds.1 = (bf16[64,512]{1,0:T(8,128)(2,1)}, bf16[64,2048]{1,0:T(8,128)(2,1)}, f32[32,128]{1,0:T(8,128)}) custom-call(bf16[512,2048]{1,0:T(8,128)(2,1)} %bitcast.2, f32[32,2048]{1,0:T(8,128)} %bitcast.4), custom_call_target="tpu_custom_call" | custom-call | tf_op jit(solution)/shard_map/power_rounds/pallas_call | solution.py:399
  147.4 4.4 %update.1 = (bf16[1,512,2048]{2,1,0:T(8,128)(2,1)}, f32[1,32,128]{2,1,0:T(8,128)}) custom-call(bf16[64,512]{1,0:T(8,128)(2,1)} %get-tuple-element.5.signed_ref, bf16[64,2048]{1,0:T(8,128)(2,1)} %get-tuple-element.6.pair_ref, bf16[512,2048]{1,0:T(8,128)(2,1)} %bitcast.3, f32[32,128]{1,0:T(8,128)} %get-tuple-element.7.factor_ref), custom_call_target="tpu_custom_call" | custom-call | tf_op jit(solution)/shard_map/update/pallas_call | solution.py:450

commit v3 on v2

--- a/solution.py
+++ b/solution.py
@@ -97,6 +97,16 @@
     far,
     summed,
     basis,
+    first_prior,
+    own_product,
+    prior_product,
+    above_product,
+    below_product,
+    both_halves,
+    partial_prior,
+    arrived_prior,
+    sum_prior,
+    sum_above,
     w_sem,
     ws_sem,
     wr_sem,
@@ -116,6 +126,16 @@
     br_sem,
     hs_sem,
     hr_sem,
+    us_sem,
+    ur_sem,
+    vs_sem,
+    vr_sem,
+    os_sem,
+    or_sem,
+    qs_sem,
+    qr_sem,
+    ds_sem,
+    dr_sem,
 ):
     blk = lax.axis_index("blk")
     shard = lax.axis_index("shard")
@@ -181,8 +201,37 @@
             shard,
         )
 
-    for c in range(CHUNKS):
-        weight_copy(c).start()
+    def lift_copy(j):
+        q = 4 * x + 2 * j + core
+        return remote(fbuf.at[q], first_prior.at[q], us_sem.at[j], ur_sem.at[j], above, shard_up)
+
+    def spread_copy(j, dx, dc):
+        t = 2 * dx + dc
+        q = 4 * x + 2 * j + core
+        return remote(
+            first_prior.at[q], first_prior.at[q], vs_sem.at[j, t], vr_sem.at[j, t], blk, mate(dx, dc)
+        )
+
+    def prior_copy(j, dx, dc):
+        t = 2 * dx + dc
+        return remote(
+            partial_prior.at[j, t],
+            arrived_prior.at[j, t],
+            qs_sem.at[j, t],
+            qr_sem.at[j, t],
+            blk,
+            mate(dx, dc),
+        )
+
+    def down_copy(j):
+        return remote(sum_prior.at[j], sum_above.at[j], ds_sem.at[j], dr_sem.at[j], below, shard_down)
+
+    own_copy = remote(own_product, below_product, os_sem.at[0], or_sem.at[0], above, shard)
+    other_copy = remote(prior_product, above_product, os_sem.at[1], or_sem.at[1], below, shard)
+
+    for j in range(2):
+        lift_copy(j).start()
+    weight_copy(0).start()
 
     def turn(part):
         start = pl.multiple_of(part * CHUNK_ROWS, CHUNK_ROWS)
@@ -191,7 +240,6 @@
                 pl.ds(start, CHUNK_ROWS), q * LANES : (q + 1) * LANES
             ].T
 
-    partial[...] = jnp.zeros_like(partial)
     for c in range(CHUNKS):
         load(c).wait()
         turn(2 * c)
@@ -270,28 +318,92 @@
 
     order = [(j, dx) for j in range(2) for dx in (2, 1, 3, 0)]
 
-    first_factor = jnp.concatenate([fbuf[q] for q in range(16)], axis=1)
-
-    def first_chunk(c, carry):
-        weight_copy(c).wait_recv()
-        turn(2 * c + 1)
-        start = pl.multiple_of(2 * CHUNK_ROWS * c, 2 * CHUNK_ROWS)
-        rows = pl.ds(start, 2 * CHUNK_ROWS)
-        own = mix(first_factor, wside[:, rows], ((1,), (0,)))
-        value = own[:, :CHUNK_ROWS] - own[:, CHUNK_ROWS:]
-        raw[0:RANK, pl.ds(pl.multiple_of(CHUNK_ROWS * c, CHUNK_ROWS), CHUNK_ROWS)] = value
-        keep_halves(value, start)
+    def own_rows_product(factors):
+        factor = jnp.concatenate([factors[q] for q in range(16)], axis=1)
+        return jnp.concatenate(
+            [
+                mix(factor, wside[:, 2 * c * CHUNK_ROWS : (2 * c + 1) * CHUNK_ROWS], ((1,), (0,)))
+                for c in range(CHUNKS)
+            ],
+            axis=1,
+        )
+
+    own_product[...] = own_rows_product(fbuf)
+    own_copy.start()
+    for j in range(2):
+        lift_copy(j).wait_recv()
+        for dx, dc in others:
+            spread_copy(j, dx, dc).start()
+    for j in range(2):
+        for dx, dc in others:
+            spread_copy(j, dx, dc).wait_recv()
+    prior_product[...] = own_rows_product(first_prior)
+    other_copy.start()
+    for c in range(1, CHUNKS):
+        weight_copy(c).start()
+    other_copy.wait_recv()
+    raw_own = own_product[...] - above_product[...]
+    raw[0:RANK, :] = raw_own
+    send_gram()
+    own_copy.wait_recv()
+    raw_prior = below_product[...] - prior_product[...]
+    for place_in, value in ((0, raw_own), (2 * RANK, -raw_prior)):
+        high = value.astype(BF16)
+        both_halves[place_in : place_in + RANK, :] = high
+        both_halves[place_in + RANK : place_in + 2 * RANK, :] = (value - high.astype(F32)).astype(BF16)
+    for j, dx in order:
+        start = pl.multiple_of(512 * lax.rem(x + dx, 4) + 256 * j, 256)
+        both = jnp.zeros((4 * RANK, 256), F32)
+        for c in range(CHUNKS):
+            here = slice(2 * c * CHUNK_ROWS, (2 * c + 1) * CHUNK_ROWS)
+            left = both_halves[:, c * CHUNK_ROWS : (c + 1) * CHUNK_ROWS]
+            both = both + mix(left, wbuf[here, pl.ds(start, 256)], ((1,), (0,)))
+        piece = both[:RANK] + both[RANK : 2 * RANK]
+        piece_prior = both[2 * RANK : 3 * RANK] + both[3 * RANK :]
+        near, away = 2 * dx + core, 2 * dx + 1 - core
+        partial_prior[j, near] = piece_prior[:, :LANES]
+        partial_prior[j, away] = piece_prior[:, LANES:]
+        partial[j, near] = piece[:, :LANES]
+        partial[j, away] = piece[:, LANES:]
+        for dc in (0, 1):
+            if dx or dc:
+                prior_copy(j, dx, dc).start()
+                part_copy(j, dx, dc).start()
+    for j in range(2):
+        total = partial_prior[j, 0]
+        for dx, dc in others:
+            prior_copy(j, dx, dc).wait_recv()
+        for t in range(1, 8):
+            total = total + arrived_prior[j, t]
+        sum_prior[j] = total
+        down_copy(j).start()
+        lift_copy(j).wait_send()
+
+    def second_start():
+        for j in range(2):
+            for dx, dc in others:
+                gather_copy(j, dx, dc).wait()
+        partial[...] = jnp.zeros_like(partial)
+
+        def chunk(c, carry):
+            weight_copy(c).wait_recv()
+            turn(2 * c + 1)
+            start = pl.multiple_of(2 * CHUNK_ROWS * c, 2 * CHUNK_ROWS)
+            rows = pl.ds(start, 2 * CHUNK_ROWS)
+            factor = jnp.concatenate([fbuf[q] for q in range(16)], axis=1)
+            own = mix(factor, wside[:, rows], ((1,), (0,)))
+            value = own[:, :CHUNK_ROWS] - own[:, CHUNK_ROWS:]
+            raw[0:RANK, pl.ds(pl.multiple_of(CHUNK_ROWS * c, CHUNK_ROWS), CHUNK_ROWS)] = value
+            keep_halves(value, start)
+            for j, dx in order:
+                for t, piece in product(rows, j, dx):
+                    partial[j, t] = partial[j, t] + piece
+            return carry
+
+        lax.fori_loop(0, CHUNKS, chunk, 0)
         for j, dx in order:
-            for t, piece in product(rows, j, dx):
-                partial[j, t] = partial[j, t] + piece
-        return carry
-
-    lax.fori_loop(0, CHUNKS, first_chunk, 0)
-    for j, dx in order:
-        send_parts(j, dx)
-    send_gram()
-    for c in range(CHUNKS):
-        weight_copy(c).wait_send()
+            send_parts(j, dx)
+        send_gram()
 
     def forward():
         own = jnp.zeros((RANK, 2 * ROWS), F32)
@@ -326,6 +438,12 @@
             for t in range(1, 8):
                 total = total + arrived[j, t]
             plane[slot, j] = total
+
+            @pl.when(k == 0)
+            def _():
+                down_copy(j).wait_recv()
+                plane[slot, j] = plane[slot, j] + sum_above[j]
+
             far_copy(slot, j).start()
         far_gram_copy(slot).wait_recv()
         lower_inv = inverse_lower(gram_plane[slot] + gram_far[slot])
@@ -359,7 +477,8 @@
         far_gram_copy(slot).wait_send()
         for j in range(2):
             far_copy(slot, j).wait_send()
-        pl.when(k < POWER - 1)(forward)
+        pl.when(k == 0)(second_start)
+        pl.when(jnp.logical_and(k > 0, k < POWER - 1))(forward)
         return carry
 
     lax.fori_loop(0, POWER, step, 0)
@@ -384,12 +503,15 @@
     basis_copy.wait_send()
     for j in range(2):
         up_copy(j).wait_send()
-
-
-def update_kernel(signed_ref, pair_ref, w_ref, factor_ref, out_ref, new_ref):
-    delta = mix(signed_ref[...], pair_ref[...], ((0,), (0,)))
-    out_ref[0] = (w_ref[...].astype(F32) + MIXING * delta).astype(BF16)
-    new_ref[0] = factor_ref[...]
+    for c in range(CHUNKS):
+        weight_copy(c).wait_send()
+    own_copy.wait_send()
+    other_copy.wait_send()
+    for j in range(2):
+        down_copy(j).wait_send()
+        for dx, dc in others:
+            spread_copy(j, dx, dc).wait_send()
+            prior_copy(j, dx, dc).wait_send()
 
 
 def on_device(weights, warm_factor):
@@ -423,6 +545,16 @@
             pltpu.VMEM((2, 2, RANK, LANES), F32),
             pltpu.VMEM((LANES, LANES), F32),
             pltpu.VMEM((RANK, ROWS), BF16),
+            pltpu.VMEM((16, RANK, LANES), BF16),
+            pltpu.VMEM((RANK, ROWS), F32),
+            pltpu.VMEM((RANK, ROWS), F32),
+            pltpu.VMEM((RANK, ROWS), F32),
+            pltpu.VMEM((RANK, ROWS), F32),
+            pltpu.VMEM((4 * RANK, ROWS), BF16),
+            pltpu.VMEM((2, 8, RANK, LANES), F32),
+            pltpu.VMEM((2, 8, RANK, LANES), F32),
+            pltpu.VMEM((2, RANK, LANES), F32),
+            pltpu.VMEM((2, RANK, LANES), F32),
             dma((CHUNKS,)),
             dma((CHUNKS,)),
             dma((CHUNKS,)),
@@ -442,31 +574,25 @@
             dma,
             dma((2, 8)),
             dma((2, 8)),
+            dma((2,)),
+            dma((2,)),
+            dma((2, 8)),
+            dma((2, 8)),
+            dma((2,)),
+            dma((2,)),
+            dma((2, 8)),
+            dma((2, 8)),
+            dma((2,)),
+            dma((2,)),
         ],
-        compiler_params=pltpu.CompilerParams(collective_id=0, has_side_effects=True),
+        compiler_params=pltpu.CompilerParams(
+            collective_id=0, has_side_effects=True, vmem_limit_bytes=48 * 2**20
+        ),
         name="power_rounds",
     )(local_weight, warm_factor[0])
-    columns = 512
-    new_weight, new_factor = pl.pallas_call(
-        update_kernel,
-        grid=(WID // columns,),
-        out_shape=(
-            jax.ShapeDtypeStruct((1, ROWS, WID), BF16),
-            jax.ShapeDtypeStruct((1, RANK, LANES), F32),
-        ),
-        in_specs=[
-            pl.BlockSpec((2 * RANK, ROWS), lambda i: (0, 0)),
-            pl.BlockSpec((2 * RANK, columns), lambda i: (0, i)),
-            pl.BlockSpec((ROWS, columns), lambda i: (0, i)),
-            pl.BlockSpec((RANK, LANES), lambda i: (0, 0)),
-        ],
-        out_specs=(
-            pl.BlockSpec((1, ROWS, columns), lambda i: (0, 0, i)),
-            pl.BlockSpec((1, RANK, LANES), lambda i: (0, 0, 0)),
-        ),
-        name="update",
-    )(signed, factor_pair, local_weight, new_factor)
-    return new_weight, new_factor
+    delta = jnp.einsum("jr,jc->rc", signed, factor_pair, preferred_element_type=F32)
+    new_weight = (local_weight.astype(F32) + MIXING * delta).astype(BF16)
+    return (new_weight[None], new_factor[None])
 
 
 def solution(mesh):

time: 152 us -> 153 us (level)
  the two profiles are of different devices: /device:TPU:1 before, /device:TPU:57 now
where the time goes in v3:
time: 153 us
  Pallas kernels  147 us (96%)
  local copies, waits for them, and re-layouts  3.14 us (2%)
  matrix products  2.05 us (1%)
    pallas_call x1, Pallas kernels, on_device(): pl.pallas_call(kernel, out_shape=(jax.ShapeDtypeStruct((2 * RANK, ROWS),...  147 us
    unnamed x5, local copies, waits for them, and re-layouts  3.14 us

profile of v3, /device:TPU:57, one launch (start us, length us, event | category | flops | bytes accessed | tf_op | source)
XLA Modules:
  0.0 152.6 jit_solution(11852002629648402606)
XLA Ops:
  0.6 0.0 copy-start
  0.6 1.6 %copy-done = bf16[1,512,2048]{2,1,0:T(8,128)(2,1)S(1)} copy-done((bf16[1,512,2048]{2,1,0:T(8,128)(2,1)S(1)}, bf16[1,512,2048]{2,1,0:T(8,128)(2,1)}, u32[]{:S(2)}) %copy-start) | copy-done | bytes 2097176
  2.2 0.0 copy-start.1
  2.2 0.9 copy-done.1
  3.2 146.8 %power_rounds.1 = (bf16[64,512]{1,0:T(8,128)(2,1)S(1)}, bf16[64,2048]{1,0:T(8,128)(2,1)S(1)}, f32[32,128]{1,0:T(8,128)S(1)}) custom-call(bf16[512,2048]{1,0:T(8,128)(2,1)S(1)} %bitcast.8, f32[32,2048]{1,0:T(8,128)S(1)} %bitcast.9), custom_call_target="tpu_custom_call" | custom-call | tf_op jit(solution)/shard_map/power_rounds/pallas_call | solution.py:521
  150.0 2.1 %fusion = bf16[1,512,2048]{2,1,0:T(8,128)(2,1)} fusion(bf16[64,512]{1,0:T(8,128)(2,1)S(1)} %get-tuple-element.5, bf16[64,2048]{1,0:T(8,128)(2,1)S(1)} %get-tuple-element.6, bf16[1,512,2048]{2,1,0:T(8,128)(2,1)S(1)} %copy-done), kind=kOutput, calls=%fused_computation.1 | convolution fusion | flops 138412032 | bytes 4521984 | tf_op jit(solution)/shard_map/jr,jc->rc/dot_general | solution.py:593
  152.0 0.6 copy.5
Async XLA Ops:
  0.6 1.6 %copy-start = (bf16[1,512,2048]{2,1,0:T(8,128)(2,1)S(1)}, bf16[1,512,2048]{2,1,0:T(8,128)(2,1)}, u32[]{:S(2)}) copy-start(bf16[1,512,2048]{2,1,0:T(8,128)(2,1)} %param.2) | copy-start | bytes 6291460
  2.2 0.9 copy-start.1

commit v4 on v3

--- a/solution.py
+++ b/solution.py
@@ -19,6 +19,8 @@
 LANES = 128
 CHUNKS = 4
 CHUNK_ROWS = ROWS // CHUNKS
+PIECES = 8
+PIECE_ROWS = ROWS // PIECES
 BLOCK = 4
 
 
@@ -190,13 +192,13 @@
     summed[...] = jnp.zeros_like(summed)
     pl.semaphore_wait(barrier, len(greeted))
 
-    def weight_copy(c):
-        rows = pl.ds(c * CHUNK_ROWS, CHUNK_ROWS)
+    def weight_copy(i):
+        first = 2 * (i // 2) * CHUNK_ROWS + CHUNK_ROWS + (i % 2) * PIECE_ROWS
         return remote(
-            w_hbm.at[rows, :],
-            wbuf.at[pl.ds((2 * c + 1) * CHUNK_ROWS, CHUNK_ROWS), :],
-            ws_sem.at[c],
-            wr_sem.at[c],
+            w_hbm.at[pl.ds(i * PIECE_ROWS, PIECE_ROWS), :],
+            wbuf.at[pl.ds(first, PIECE_ROWS), :],
+            ws_sem.at[i],
+            wr_sem.at[i],
             below,
             shard,
         )
@@ -231,7 +233,8 @@
 
     for j in range(2):
         lift_copy(j).start()
-    weight_copy(0).start()
+    for i in (0, 1):
+        weight_copy(i).start()
 
     def turn(part):
         start = pl.multiple_of(part * CHUNK_ROWS, CHUNK_ROWS)
@@ -339,8 +342,8 @@
             spread_copy(j, dx, dc).wait_recv()
     prior_product[...] = own_rows_product(first_prior)
     other_copy.start()
-    for c in range(1, CHUNKS):
-        weight_copy(c).start()
+    for i in (2, 3):
+        weight_copy(i).start()
     other_copy.wait_recv()
     raw_own = own_product[...] - above_product[...]
     raw[0:RANK, :] = raw_own
@@ -369,6 +372,8 @@
             if dx or dc:
                 prior_copy(j, dx, dc).start()
                 part_copy(j, dx, dc).start()
+    for i in (4, 5):
+        weight_copy(i).start()
     for j in range(2):
         total = partial_prior[j, 0]
         for dx, dc in others:
@@ -378,6 +383,8 @@
         sum_prior[j] = total
         down_copy(j).start()
         lift_copy(j).wait_send()
+    for i in (6,):
+        weight_copy(i).start()
 
     def second_start():
         for j in range(2):
@@ -386,7 +393,8 @@
         partial[...] = jnp.zeros_like(partial)
 
         def chunk(c, carry):
-            weight_copy(c).wait_recv()
+            weight_copy(2 * c).wait_recv()
+            weight_copy(2 * c + 1).wait_recv()
             turn(2 * c + 1)
             start = pl.multiple_of(2 * CHUNK_ROWS * c, 2 * CHUNK_ROWS)
             rows = pl.ds(start, 2 * CHUNK_ROWS)
@@ -445,6 +453,12 @@
                 plane[slot, j] = plane[slot, j] + sum_above[j]
 
             far_copy(slot, j).start()
+
+        @pl.when(k == 0)
+        def _():
+            for i in (7,):
+                weight_copy(i).start()
+
         far_gram_copy(slot).wait_recv()
         lower_inv = inverse_lower(gram_plane[slot] + gram_far[slot])
 
@@ -503,8 +517,8 @@
     basis_copy.wait_send()
     for j in range(2):
         up_copy(j).wait_send()
-    for c in range(CHUNKS):
-        weight_copy(c).wait_send()
+    for i in range(PIECES):
+        weight_copy(i).wait_send()
     own_copy.wait_send()
     other_copy.wait_send()
     for j in range(2):
@@ -556,8 +570,8 @@
             pltpu.VMEM((2, RANK, LANES), F32),
             pltpu.VMEM((2, RANK, LANES), F32),
             dma((CHUNKS,)),
-            dma((CHUNKS,)),
-            dma((CHUNKS,)),
+            dma((PIECES,)),
+            dma((PIECES,)),
             dma((8,)),
             dma((8,)),
             dma((2, 8)),

time: 153 us -> 145 us (0.948)
  the two profiles are of different devices: /device:TPU:57 before, /device:TPU:89 now
where the time goes in v4:
time: 145 us
  Pallas kernels  139 us (96%)
  local copies, waits for them, and re-layouts  3.14 us (2%)
  matrix products  2.05 us (1%)
    pallas_call x1, Pallas kernels, on_device(): pl.pallas_call(kernel, out_shape=(jax.ShapeDtypeStruct((2 * RANK, ROWS),...  139 us
    unnamed x5, local copies, waits for them, and re-layouts  3.14 us

profile of v4, /device:TPU:89, one launch (start us, length us, event | category | flops | bytes accessed | tf_op | source)
XLA Modules:
  0.0 144.7 jit_solution(15039340605532069853)
XLA Ops:
  0.6 0.0 copy-start
  0.6 1.6 %copy-done = bf16[1,512,2048]{2,1,0:T(8,128)(2,1)S(1)} copy-done((bf16[1,512,2048]{2,1,0:T(8,128)(2,1)S(1)}, bf16[1,512,2048]{2,1,0:T(8,128)(2,1)}, u32[]{:S(2)}) %copy-start) | copy-done | bytes 2097176
  2.2 0.0 copy-start.1
  2.2 0.9 copy-done.1
  3.2 138.9 %power_rounds.1 = (bf16[64,512]{1,0:T(8,128)(2,1)S(1)}, bf16[64,2048]{1,0:T(8,128)(2,1)S(1)}, f32[32,128]{1,0:T(8,128)S(1)}) custom-call(bf16[512,2048]{1,0:T(8,128)(2,1)S(1)} %bitcast.8, f32[32,2048]{1,0:T(8,128)S(1)} %bitcast.9), custom_call_target="tpu_custom_call" | custom-call | tf_op jit(solution)/shard_map/power_rounds/pallas_call | solution.py:535
  142.0 2.1 %fusion = bf16[1,512,2048]{2,1,0:T(8,128)(2,1)} fusion(bf16[64,512]{1,0:T(8,128)(2,1)S(1)} %get-tuple-element.5, bf16[64,2048]{1,0:T(8,128)(2,1)S(1)} %get-tuple-element.6, bf16[1,512,2048]{2,1,0:T(8,128)(2,1)S(1)} %copy-done), kind=kOutput, calls=%fused_computation.1 | convolution fusion | flops 138412032 | bytes 4521984 | tf_op jit(solution)/shard_map/jr,jc->rc/dot_general | solution.py:607
  144.1 0.6 copy.5
Async XLA Ops:
  0.6 1.6 %copy-start = (bf16[1,512,2048]{2,1,0:T(8,128)(2,1)S(1)}, bf16[1,512,2048]{2,1,0:T(8,128)(2,1)}, u32[]{:S(2)}) copy-start(bf16[1,512,2048]{2,1,0:T(8,128)(2,1)} %param.2) | copy-start | bytes 6291460
  2.2 0.9 copy-start.1

commit v5 on v4

--- a/solution.py
+++ b/solution.py
@@ -21,7 +21,8 @@
 CHUNK_ROWS = ROWS // CHUNKS
 PIECES = 8
 PIECE_ROWS = ROWS // PIECES
-BLOCK = 4
+AWAY = (2, 1, 3, 0)
+BLOCK = 8
 
 
 def mix(a, b, dims):
@@ -319,7 +320,7 @@
             if dx or dc:
                 part_copy(j, dx, dc).start()
 
-    order = [(j, dx) for j in range(2) for dx in (2, 1, 3, 0)]
+    order = [(j, dx) for j in range(2) for dx in AWAY]
 
     def own_rows_product(factors):
         factor = jnp.concatenate([factors[q] for q in range(16)], axis=1)
@@ -354,24 +355,24 @@
         high = value.astype(BF16)
         both_halves[place_in : place_in + RANK, :] = high
         both_halves[place_in + RANK : place_in + 2 * RANK, :] = (value - high.astype(F32)).astype(BF16)
-    for j, dx in order:
-        start = pl.multiple_of(512 * lax.rem(x + dx, 4) + 256 * j, 256)
-        both = jnp.zeros((4 * RANK, 256), F32)
-        for c in range(CHUNKS):
-            here = slice(2 * c * CHUNK_ROWS, (2 * c + 1) * CHUNK_ROWS)
-            left = both_halves[:, c * CHUNK_ROWS : (c + 1) * CHUNK_ROWS]
-            both = both + mix(left, wbuf[here, pl.ds(start, 256)], ((1,), (0,)))
-        piece = both[:RANK] + both[RANK : 2 * RANK]
-        piece_prior = both[2 * RANK : 3 * RANK] + both[3 * RANK :]
-        near, away = 2 * dx + core, 2 * dx + 1 - core
-        partial_prior[j, near] = piece_prior[:, :LANES]
-        partial_prior[j, away] = piece_prior[:, LANES:]
-        partial[j, near] = piece[:, :LANES]
-        partial[j, away] = piece[:, LANES:]
-        for dc in (0, 1):
-            if dx or dc:
-                prior_copy(j, dx, dc).start()
-                part_copy(j, dx, dc).start()
+    for j in range(2):
+        for dx in AWAY:
+            start = pl.multiple_of(512 * lax.rem(x + dx, 4) + 256 * j, 256)
+            both = jnp.zeros((4 * RANK, 256), F32)
+            for c in range(CHUNKS):
+                here = slice(2 * c * CHUNK_ROWS, (2 * c + 1) * CHUNK_ROWS)
+                left = both_halves[:, c * CHUNK_ROWS : (c + 1) * CHUNK_ROWS]
+                both = both + mix(left, wbuf[here, pl.ds(start, 256)], ((1,), (0,)))
+            piece = both[:RANK] + both[RANK : 2 * RANK]
+            piece_prior = both[2 * RANK : 3 * RANK] + both[3 * RANK :]
+            near, away = 2 * dx + core, 2 * dx + 1 - core
+            partial_prior[j, near] = piece_prior[:, :LANES]
+            partial_prior[j, away] = piece_prior[:, LANES:]
+            partial[j, near] = piece[:, :LANES]
+            partial[j, away] = piece[:, LANES:]
+        for dx, dc in others:
+            prior_copy(j, dx, dc).start()
+            part_copy(j, dx, dc).start()
     for i in (4, 5):
         weight_copy(i).start()
     for j in range(2):
@@ -428,10 +429,12 @@
             raw[0:RANK, CHUNK_ROWS * c : CHUNK_ROWS * (c + 1)] = value
             keep_halves(value, start)
         send_gram()
-        for j, dx in order:
-            for t, piece in product(slice(None), j, dx):
-                partial[j, t] = piece
-            send_parts(j, dx)
+        for j in range(2):
+            for dx in AWAY:
+                for t, piece in product(slice(None), j, dx):
+                    partial[j, t] = piece
+            for dx in AWAY:
+                send_parts(j, dx)
 
     def step(k, carry):
         slot = lax.rem(k, 2)

time: 145 us -> 144 us (level)
  the two profiles are of different devices: /device:TPU:89 before, /device:TPU:65 now
where the time goes in v5:
time: 144 us
  Pallas kernels  138 us (96%)
  local copies, waits for them, and re-layouts  3.14 us (2%)
  matrix products  2.05 us (1%)
    pallas_call x1, Pallas kernels, on_device(): pl.pallas_call(kernel, out_shape=(jax.ShapeDtypeStruct((2 * RANK, ROWS),...  138 us
    unnamed x5, local copies, waits for them, and re-layouts  3.14 us

profile of v5, /device:TPU:65, one launch (start us, length us, event | category | flops | bytes accessed | tf_op | source)
XLA Modules:
  0.0 144.1 jit_solution(9756556860069824052)
XLA Ops:
  0.6 0.0 copy-start
  0.6 1.6 %copy-done = bf16[1,512,2048]{2,1,0:T(8,128)(2,1)S(1)} copy-done((bf16[1,512,2048]{2,1,0:T(8,128)(2,1)S(1)}, bf16[1,512,2048]{2,1,0:T(8,128)(2,1)}, u32[]{:S(2)}) %copy-start) | copy-done | bytes 2097176
  2.2 0.0 copy-start.1
  2.2 0.9 copy-done.1
  3.2 138.3 %power_rounds.1 = (bf16[64,512]{1,0:T(8,128)(2,1)S(1)}, bf16[64,2048]{1,0:T(8,128)(2,1)S(1)}, f32[32,128]{1,0:T(8,128)S(1)}) custom-call(bf16[512,2048]{1,0:T(8,128)(2,1)S(1)} %bitcast.8, f32[32,2048]{1,0:T(8,128)S(1)} %bitcast.9), custom_call_target="tpu_custom_call" | custom-call | tf_op jit(solution)/shard_map/power_rounds/pallas_call | solution.py:538
  141.5 2.0 %fusion = bf16[1,512,2048]{2,1,0:T(8,128)(2,1)} fusion(bf16[64,512]{1,0:T(8,128)(2,1)S(1)} %get-tuple-element.5, bf16[64,2048]{1,0:T(8,128)(2,1)S(1)} %get-tuple-element.6, bf16[1,512,2048]{2,1,0:T(8,128)(2,1)S(1)} %copy-done), kind=kOutput, calls=%fused_computation.1 | convolution fusion | flops 138412032 | bytes 4521984 | tf_op jit(solution)/shard_map/jr,jc->rc/dot_general | solution.py:610
  143.5 0.6 copy.5
Async XLA Ops:
  0.6 1.6 %copy-start = (bf16[1,512,2048]{2,1,0:T(8,128)(2,1)S(1)}, bf16[1,512,2048]{2,1,0:T(8,128)(2,1)}, u32[]{:S(2)}) copy-start(bf16[1,512,2048]{2,1,0:T(8,128)(2,1)} %param.2) | copy-start | bytes 6291460
  2.2 0.9 copy-start.1
